TPU v7x, 512 devices: a whole 4x4x16 slice. The times are simulated.
512 devices in a mesh: dp: 64 (over y_hi, z, core), tensor: 8 (over x, y_lo).
Axes of the slice: x: 4, y: 4 (y_hi: 2, y_lo: 2; y = y_hi * 2 + y_lo), z: 16, core: 2. Of those that a mesh axis runs over, the one named last changes fastest.
Arguments:
- queries: bfloat16 [2048, 5120], P('dp', 'tensor'), may hold values from -8 to 8
- new_keys: bfloat16 [2048, 5120], P('dp', 'tensor'), may hold values from -8 to 8
- new_values: bfloat16 [2048, 5120], P('dp', 'tensor'), may hold values from -6 to 6
- key_pool: bfloat16 [1024, 16, 5120], P('dp', None, 'tensor'), may hold values from -6 to 6
- value_pool: bfloat16 [1024, 16, 5120], P('dp', None, 'tensor'), may hold values from -6 to 6
- page_table: int32 [128, 16], P('dp'), may hold values from 0 to 15, as said below
- lengths: int32 [128], P('dp'), may hold values from 1 to 240, as said below
- timesteps: int32 [128], replicated, may hold values from 0 to 49
- gate_table: float32 [50, 5120], P(None, 'dp'), may hold values from -4 to 4
- out_weight: bfloat16 [5120, 5120], P('tensor', 'dp'), may hold values from -0.078125 to 0.078125
- residual: bfloat16 [32, 64, 5120], P('tensor', None, 'dp'), may hold values from -1.5 to 1.5
Outputs:
- mixed: bfloat16 [32, 64, 5120], P('tensor', None, 'dp')
Inputs may be any that keep to these rules, and one draw needn't show every extreme that they name: `page_table`: ids of pages within the 16-page pool of the request's own group; the first ceil(lengths[r] / 16) entries of the requests of one group are distinct pages, and together they take at most 16 pages; in every draw some group takes all 16. `lengths`: some request has exactly 240 cached positions in every draw.
All inputs are finite; a program needn't handle non-finite values.
Results may differ from a plain program's by a relative error of at most 0.0054.
Values may be sent and summed in bfloat16 or wider, within the bound.
No kernel may reach another device: no remote copies, remote signals or barrier semaphores. Data moves between devices by JAX's collectives and lax.ppermute only.
A program may use at most 64 MiB of HBM per device.

v0:
```python
import math
import jax
import jax.numpy as jnp
from jax import lax
from jax.sharding import Mesh
from jax.sharding import PartitionSpec as P

HEAD = 128


def attend(queries, new_keys, new_values, key_pool, value_pool, page_table, lengths):
    req_dev = page_table.shape[0]
    pages, page_len, width = key_pool.shape
    tok_count = queries.shape[0]
    new_count = tok_count // req_dev
    heads_dev = width // HEAD
    cached = pages * page_len
    keys_all = jnp.concatenate(
        [
            key_pool[page_table].reshape(req_dev, cached, width),
            new_keys.reshape(req_dev, new_count, width),
        ],
        axis=1,
    )
    vals_all = jnp.concatenate(
        [
            value_pool[page_table].reshape(req_dev, cached, width),
            new_values.reshape(req_dev, new_count, width),
        ],
        axis=1,
    )
    keys_all = keys_all.reshape(req_dev, cached + new_count, heads_dev, HEAD)
    vals_all = vals_all.reshape(req_dev, cached + new_count, heads_dev, HEAD)
    query_four = queries.reshape(req_dev, new_count, heads_dev, HEAD)
    scores = jnp.einsum(
        "rqhd,rkhd->rhqk", query_four, keys_all, preferred_element_type=jnp.float32
    ) * (1.0 / math.sqrt(HEAD))
    position = jnp.arange(cached + new_count)
    visible = (position[None, :] < lengths[:, None]) | (position[None, :] >= cached)
    scores = jnp.where(visible[:, None, None, :], scores, jnp.float32(-1e30))
    top = jnp.max(scores, axis=-1, keepdims=True)
    expd = jnp.exp(scores - top)
    probs = (expd / jnp.sum(expd, axis=-1, keepdims=True)).astype(jnp.bfloat16)
    mixed_heads = jnp.einsum("rhqk,rkhd->rqhd", probs, vals_all, preferred_element_type=jnp.float32)
    return mixed_heads.astype(jnp.bfloat16).reshape(tok_count, width)


def per_device(
    queries,
    new_keys,
    new_values,
    key_pool,
    value_pool,
    page_table,
    lengths,
    timesteps,
    gate_table,
    out_weight,
    residual,
):
    req_dev = page_table.shape[0]
    group_tok = queries.shape[0]
    new_count = group_tok // req_dev
    share = residual.shape[0]
    groups = residual.shape[1]
    col_count = out_weight.shape[1]
    y_hi, z_len, cores = (lax.axis_size(name) for name in ("y_hi", "z", "core"))
    tensor_len = lax.axis_size("x") * lax.axis_size("y_lo")
    weight = lax.all_gather(out_weight, ("y_hi", "core"), axis=1, tiled=True)
    attn = attend(queries, new_keys, new_values, key_pool, value_pool, page_table, lengths)
    attn_all = lax.all_gather(attn, "z", axis=0, tiled=True)
    partial = jnp.dot(attn_all, weight, preferred_element_type=jnp.float32).astype(jnp.bfloat16)
    blocks = partial.reshape(z_len, tensor_len, share, y_hi * cores, col_count)
    blocks = blocks.transpose(3, 1, 0, 2, 4).reshape(-1, z_len, share, col_count)
    arrived = lax.all_to_all(blocks, ("y_hi", "core", "x", "y_lo"), 0, 0, tiled=True)
    arrived = arrived.reshape(y_hi, cores, tensor_len, z_len, share, col_count)
    branch = jnp.sum(arrived.astype(jnp.float32), axis=2)
    branch = branch.transpose(3, 0, 2, 1, 4).reshape(share, groups, col_count)
    tensor_at = lax.axis_index(("x", "y_lo"))
    local_rows = tensor_at * share + jnp.arange(share, dtype=jnp.int32)
    request_at = (
        jnp.arange(groups, dtype=jnp.int32)[None, :] * req_dev + (local_rows // new_count)[:, None]
    )
    step_at = timesteps[request_at]
    onehot = (
        step_at[:, :, None] == jnp.arange(gate_table.shape[0], dtype=jnp.int32)[None, None, :]
    ).astype(jnp.float32)
    gate = jnp.einsum("tgs,sc->tgc", onehot, gate_table, precision=lax.Precision.HIGHEST)
    return (residual.astype(jnp.float32) + gate * branch).astype(jnp.bfloat16)


def solution(mesh):
    dp = ("y_hi", "z", "core")
    tensor = ("x", "y_lo")
    split = Mesh(mesh.devices.reshape(2, -1, 2, 4, 2), dp + tensor)
    placed = (
        P(dp, tensor),
        P(dp, tensor),
        P(dp, tensor),
        P(dp, None, tensor),
        P(dp, None, tensor),
        P(dp, None),
        P(dp),
        P(),
        P(None, dp),
        P(tensor, dp),
        P(tensor, None, dp),
    )
    return jax.shard_map(
        per_device, mesh=split, in_specs=placed, out_specs=P(tensor, None, dp), check_vma=False
    )
```

profile of v0, /device:TPU:1, one launch (start us, length us, event | category | flops | bytes accessed | tf_op | source)
XLA Modules:
  0.0 78.0 jit_solution(498488600279138065)
XLA Ops:
  0.0 0.9 %concatenate.17 = bf16[2,16,5,128]{3,2,1,0:T(8,128)(2,1)S(1)} reshape(bf16[32,640]{1,0:T(8,128)(2,1)} %param.13) | data formatting | bytes 81920 | tf_op jit(solution)/shard_map/concatenate | solution.py:25
  0.9 0.7 compare_select_fusion.1
  1.7 0.7 gather_fusion.1
  2.4 0.7 concatenate.16
  3.1 0.1 copy.21
  3.2 0.6 copy-done.5
  4.0 0.1 copy-done.2
  4.1 0.7 gather_fusion.2
  4.8 0.7 concatenate.19
  5.7 0.6 copy-done.6
  6.5 0.5 fusion.48
  6.9 0.5 fusion.7
  7.6 33.5 %all_gather.6 = bf16[512,640]{1,0:T(8,128)(2,1)S(1)} all-gather(bf16[32,640]{1,0:T(8,128)(2,1)S(1)} %bitcast.37), channel_id=1, replica_groups=mesh['y_hi'=2,'z'=16,'core'=2,'x'=4,'y_lo'=2] {'z'}, dimensions={0}, use_global_device_ids=true | all-gather | bytes 696320 | tf_op jit(solution)/shard_map/all_gather | solution.py:71
  41.0 15.7 %all_gather.7 = bf16[640,320]{0,1:T(8,128)(2,1)S(1)} all-gather(bf16[640,80]{0,1:T(8,128)(2,1)S(1)} %copy-done.3), channel_id=1, replica_groups=mesh['y_hi'=2,'z'=16,'core'=2,'x'=4,'y_lo'=2] {'y_hi','core'}, dimensions={1}, use_global_device_ids=true | all-gather | bytes 512000 | tf_op jit(solution)/shard_map/all_gather | solution.py:69
  56.7 0.4 convolution_convert_fusion
  57.2 0.2 copy.27
  57.4 0.3 reshape.147
  57.8 1.1 %copy.28 = bf16[4,8,16,4,80]{4,2,3,1,0:T(8,128)(2,1)} copy(bf16[4,8,16,4,80]{4,0,3,1,2:T(4,128)(2,1)S(1)} %bitcast.33) | data formatting | bytes 655360 | tf_op jit(solution)/shard_map/transpose | solution.py:74
  58.9 6.7 %all-to-all-start = ((bf16[32,16,4,80]{3,1,2,0:T(8,128)(2,1)}), bf16[32,16,4,80]{3,1,2,0:T(8,128)(2,1)S(1)}, u32[]{:S(2)}, u32[]{:S(2)}) async-start(bf16[32,16,4,80]{3,1,2,0:T(8,128)(2,1)} %bitcast.4), calls=%async_computation | async-start | bytes 1048576 | tf_op jit(solution)/shard_map/all_to_all | solution.py:75
  65.8 1.9 %gather_fusion = s32[256]{0:T(256)S(1)} fusion(s32[128]{0:T(128)S(1)} %copy-done.1, s32[1024]{0:T(1024)S(1)} %pad_clamp_fusion.1), kind=kCustom, calls=%fused_computation | custom fusion | bytes 3072 | tf_op jit(solution)/shard_map/gather | solution.py:84
  67.8 9.0 %all-to-all-done = bf16[32,16,4,80]{3,1,2,0:T(8,128)(2,1)S(1)} async-done(((bf16[32,16,4,80]{3,1,2,0:T(8,128)(2,1)}), bf16[32,16,4,80]{3,1,2,0:T(8,128)(2,1)S(1)}, u32[]{:S(2)}, u32[]{:S(2)}) %all-to-all-start) | async-done | bytes 327712 | tf_op jit(solution)/shard_map/all_to_all | solution.py:75
  76.8 0.1 convert_reduce_fusion
  76.9 0.1 copy.29
  77.0 0.9 %fusion.6 = bf16[4,64,80]{2,1,0:T(8,128)(2,1)} fusion(f32[4,64,80]{2,1,0:T(8,128)S(1)} %bitcast.35, bf16[4,64,80]{2,1,0:T(8,128)(2,1)S(1)} %copy-done.4, s32[4,64]{1,0:T(4,128)S(1)} %reshape.152, f32[50,80]{1,0:T(8,128)S(1)} %copy-done.7), kind=kOutput, calls=%fused_computation.12 | convolution fusion | flops 12382720 | bytes 180864 | tf_op jit(solution)/shard_map/tgs,sc->tgc/dot_general | solution.py:88
  (32 shorter events, 0.8 us)
Async XLA Ops:
  0.0 1.7 %copy-start = (bf16[16,16,640]{2,1,0:T(8,128)(2,1)S(1)}, bf16[16,16,640]{2,1,0:T(8,128)(2,1)}, u32[]{:S(2)}) copy-start(bf16[16,16,640]{2,1,0:T(8,128)(2,1)} %param.15) | copy-start | bytes 983044
  3.1 0.8 %copy-start.5 = (bf16[32,640]{1,0:T(8,128)(2,1)S(1)}, bf16[32,640]{1,0:T(8,128)(2,1)}, u32[]{:S(2)}) copy-start(bf16[32,640]{1,0:T(8,128)(2,1)} %param.12) | copy-start | bytes 122884
  3.1 1.0 %copy-start.2 = (bf16[16,16,640]{2,1,0:T(8,128)(2,1)S(1)}, bf16[16,16,640]{2,1,0:T(8,128)(2,1)}, u32[]{:S(2)}) copy-start(bf16[16,16,640]{2,1,0:T(8,128)(2,1)} %param.14) | copy-start | bytes 983044
  5.5 0.8 %copy-start.6 = (bf16[32,640]{1,0:T(8,128)(2,1)S(1)}, bf16[32,640]{1,0:T(8,128)(2,1)}, u32[]{:S(2)}) copy-start(bf16[32,640]{1,0:T(8,128)(2,1)} %param.11) | copy-start | bytes 122884
  5.5 0.8 %copy-start.8 = (s32[2]{0:T(128)S(1)}, s32[2]{0:T(128)}, u32[]{:S(2)}) copy-start(s32[2]{0:T(128)} %param.17) | copy-start | bytes 28
  6.9 34.1 %copy-start.3 = (bf16[640,80]{0,1:T(8,128)(2,1)S(1)}, bf16[640,80]{0,1:T(8,128)(2,1)}, u32[]{:S(2)}) copy-start(bf16[640,80]{0,1:T(8,128)(2,1)} %param.20) | copy-start | bytes 307204
  57.8 8.1 %copy-start.1 = (s32[128]{0:T(128)S(1)}, s32[128]{0:T(128)}, u32[]{:S(2)}) copy-start(s32[128]{0:T(128)} %param.18) | copy-start | bytes 1540
  58.9 17.9 %all-to-all-start = ((bf16[32,16,4,80]{3,1,2,0:T(8,128)(2,1)}), bf16[32,16,4,80]{3,1,2,0:T(8,128)(2,1)S(1)}, u32[]{:S(2)}, u32[]{:S(2)}) async-start(bf16[32,16,4,80]{3,1,2,0:T(8,128)(2,1)} %bitcast.4), calls=%async_computation | async-start | bytes 1048576 | tf_op jit(solution)/shard_map/all_to_all | solution.py:75
  65.8 11.2 %copy-start.4 = (bf16[4,64,80]{2,1,0:T(8,128)(2,1)S(1)}, bf16[4,64,80]{2,1,0:T(8,128)(2,1)}, u32[]{:S(2)}) copy-start(bf16[4,64,80]{2,1,0:T(8,128)(2,1)} %param.21) | copy-start | bytes 122884
  65.8 11.2 %copy-start.7 = (f32[50,80]{1,0:T(8,128)S(1)}, f32[50,80]{1,0:T(8,128)}, u32[]{:S(2)}) copy-start(f32[50,80]{1,0:T(8,128)} %param.19) | copy-start | bytes 48004
where the time goes:
time: 78.3 us; the launch traced here: 78 us
  blocking collectives  49.2 us (63%)
  local copies, waits for them, and re-layouts  9.44 us (12%)
  waiting for transfers between devices  9 us (11%)
  starting transfers between devices  6.69 us (9%)
  matrix products  2.42 us (3%)
  other arithmetic  0.98 us (1%)
    all_gather x1, blocking collectives, per_device(): attn_all = lax.all_gather(attn, 'z', axis=0, tiled=True)  33.5 us
    all_gather x1, blocking collectives, per_device(): weight = lax.all_gather(out_weight, ('y_hi', 'core'), axis=1, tiled=True)  15.7 us
    all_to_all x1, waiting for transfers between devices, per_device(): lax.all_to_all(blocks, ('y_hi', 'core', 'x', 'y_lo'), 0, 0, tiled=True)  9 us
    all_to_all x1, starting transfers between devices, per_device(): lax.all_to_all(blocks, ('y_hi', 'core', 'x', 'y_lo'), 0, 0, tiled=True)  6.69 us
    gather x2, local copies, waits for them, and re-layouts, per_device(): step_at = timesteps[request_at]  1.95 us
    concatenate x4, local copies, waits for them, and re-layouts, attend(): jnp.concatenate([value_pool[page_table].reshape(req_dev, cached, width),...  1.73 us
  transfers between devices with their start and end apart: 1, of which 1 were waited for; matrix products, arithmetic and copies ran while one was open for 3% of the time, Pallas kernels for 0%

commit v1 on v0

--- a/solution.py
+++ b/solution.py
@@ -66,7 +66,8 @@
     col_count = out_weight.shape[1]
     y_hi, z_len, cores = (lax.axis_size(name) for name in ("y_hi", "z", "core"))
     tensor_len = lax.axis_size("x") * lax.axis_size("y_lo")
-    weight = lax.all_gather(out_weight, ("y_hi", "core"), axis=1, tiled=True)
+    repeated = jnp.stack([out_weight] * lax.axis_size(("y_hi", "core")))
+    weight = jnp.concatenate(lax.all_to_all(repeated, ("y_hi", "core"), 0, 0), axis=1)
     attn = attend(queries, new_keys, new_values, key_pool, value_pool, page_table, lengths)
     attn_all = lax.all_gather(attn, "z", axis=0, tiled=True)
     partial = jnp.dot(attn_all, weight, preferred_element_type=jnp.float32).astype(jnp.bfloat16)

time: 78.3 us -> 75 us (0.958)
  blocking collectives: 49.2 us -> 27.6 us
  starting transfers between devices: 6.69 us -> 24.7 us
  local copies, waits for them, and re-layouts: 9.44 us -> 10.3 us
    all_gather x1 -> x0, blocking collectives: 15.7 us -> none  [per_device(): weight = lax.all_gather(out_weight, ('y_hi', 'core'), axis=1, tiled=True)]
    all_to_all x0 -> x1, starting transfers between devices: none -> 10.3 us  [per_device(): lax.all_to_all(repeated, ('y_hi', 'core'), 0, 0)]
    all_to_all x1, starting transfers between devices: 6.69 us -> 14.5 us  [per_device(): lax.all_to_all(blocks, ('y_hi', 'core', 'x', 'y_lo'), 0, 0, tiled=True)]
    all_gather x1, blocking collectives: 33.5 us -> 27.6 us  [per_device(): attn_all = lax.all_gather(attn, 'z', axis=0, tiled=True)]
    another operation x0 -> x1, local copies, waits for them, and re-layouts: none -> 1.73 us  [per_device(): repeated = jnp.stack([out_weight] * lax.axis_size(('y_hi', 'core')))]
    concatenate x4, local copies, waits for them, and re-layouts: 1.73 us -> 0.9 us  [attend(): jnp.concatenate([value_pool[page_table].reshape(req_dev, cached, width),...]
  transfers between devices with their start and end apart: 1 -> 2, of which waited for: 1 -> 1; matrix products, arithmetic and copies ran while one was open for 3% -> 9% of each run, Pallas kernels for 0% -> 0%
where the time goes in v1:
time: 75 us; the launch traced here: 74.7 us
  blocking collectives  27.6 us (37%)
  starting transfers between devices  24.7 us (33%)
  local copies, waits for them, and re-layouts  10.3 us (14%)
  waiting for transfers between devices  9.04 us (12%)
  matrix products  2.43 us (3%)
    all_gather x1, blocking collectives, per_device(): attn_all = lax.all_gather(attn, 'z', axis=0, tiled=True)  27.6 us
    all_to_all x1, starting transfers between devices, per_device(): lax.all_to_all(blocks, ('y_hi', 'core', 'x', 'y_lo'), 0, 0, tiled=True)  14.5 us
    all_to_all x1, starting transfers between devices, per_device(): lax.all_to_all(repeated, ('y_hi', 'core'), 0, 0)  10.3 us
    all_to_all x1, waiting for transfers between devices, per_device(): lax.all_to_all(blocks, ('y_hi', 'core', 'x', 'y_lo'), 0, 0, tiled=True)  9.04 us
    gather x2, local copies, waits for them, and re-layouts, per_device(): step_at = timesteps[request_at]  1.95 us
    another operation x1, local copies, waits for them, and re-layouts, per_device(): repeated = jnp.stack([out_weight] * lax.axis_size(('y_hi', 'core')))  1.73 us
  transfers between devices with their start and end apart: 2, of which 1 were waited for; matrix products, arithmetic and copies ran while one was open for 9% of the time, Pallas kernels for 0%

profile of v1, /device:TPU:1, one launch (start us, length us, event | category | flops | bytes accessed | tf_op | source)
XLA Modules:
  0.0 74.7 jit_solution(7405348265615091282)
XLA Ops:
  0.0 1.7 %stack.2 = bf16[4,640,80]{1,2,0:T(8,128)(2,1)} broadcast(bf16[640,80]{0,1:T(8,128)(2,1)} %param.20), dimensions={1,2} | broadcast | bytes 512000 | tf_op jit(solution)/shard_map/stack | solution.py:69
  1.7 10.3 %all-to-all-start = ((bf16[4,640,80]{1,2,0:T(8,128)(2,1)}), bf16[4,640,80]{1,2,0:T(8,128)(2,1)S(1)}, u32[]{:S(2)}, u32[]{:S(2)}) async-start(bf16[4,640,80]{1,2,0:T(8,128)(2,1)} %stack.2), calls=%async_computation | async-start | bytes 819200 | tf_op jit(solution)/shard_map/all_to_all | solution.py:70
  12.2 0.7 gather_fusion.1
  12.9 0.7 concatenate.16
  13.7 0.1 copy.22
  13.8 0.6 copy-done.5
  14.5 0.1 copy-done.2
  14.6 0.7 gather_fusion.2
  15.3 0.7 concatenate.19
  16.1 0.1 copy.24
  16.2 0.6 copy-done.6
  17.0 0.5 fusion.48
  17.5 0.5 fusion.7
  18.1 27.6 %all_gather.3 = bf16[512,640]{1,0:T(8,128)(2,1)S(1)} all-gather(bf16[32,640]{1,0:T(8,128)(2,1)S(1)} %bitcast.41), channel_id=1, replica_groups=mesh['y_hi'=2,'z'=16,'core'=2,'x'=4,'y_lo'=2] {'z'}, dimensions={0}, use_global_device_ids=true | all-gather | bytes 696320 | tf_op jit(solution)/shard_map/all_gather | solution.py:72
  45.7 0.4 convolution_convert_fusion
  46.1 0.2 copy.28
  46.3 0.3 reshape.157
  46.7 1.1 %copy.29 = bf16[4,8,16,4,80]{4,2,3,1,0:T(8,128)(2,1)} copy(bf16[4,8,16,4,80]{4,0,3,1,2:T(4,128)(2,1)S(1)} %bitcast.36) | data formatting | bytes 655360 | tf_op jit(solution)/shard_map/transpose | solution.py:75
  47.8 14.5 %all-to-all-start.1 = ((bf16[32,16,4,80]{3,1,2,0:T(8,128)(2,1)}), bf16[32,16,4,80]{3,1,2,0:T(8,128)(2,1)S(1)}, u32[]{:S(2)}, u32[]{:S(2)}) async-start(bf16[32,16,4,80]{3,1,2,0:T(8,128)(2,1)} %bitcast.6), calls=%async_computation.1 | async-start | bytes 1048576 | tf_op jit(solution)/shard_map/all_to_all | solution.py:76
  62.5 1.9 %gather_fusion = s32[256]{0:T(256)S(1)} fusion(s32[128]{0:T(128)S(1)} %copy-done.1, s32[1024]{0:T(1024)S(1)} %pad_clamp_fusion.1), kind=kCustom, calls=%fused_computation | custom fusion | bytes 3072 | tf_op jit(solution)/shard_map/gather | solution.py:85
  64.5 9.0 %all-to-all-done.1 = bf16[32,16,4,80]{3,1,2,0:T(8,128)(2,1)S(1)} async-done(((bf16[32,16,4,80]{3,1,2,0:T(8,128)(2,1)}), bf16[32,16,4,80]{3,1,2,0:T(8,128)(2,1)S(1)}, u32[]{:S(2)}, u32[]{:S(2)}) %all-to-all-start.1) | async-done | bytes 327712 | tf_op jit(solution)/shard_map/all_to_all | solution.py:76
  73.5 0.1 convert_reduce_fusion
  73.6 0.1 copy.30
  73.7 0.9 %fusion.6 = bf16[4,64,80]{2,1,0:T(8,128)(2,1)} fusion(f32[4,64,80]{2,1,0:T(8,128)S(1)} %bitcast.39, bf16[4,64,80]{2,1,0:T(8,128)(2,1)S(1)} %copy-done.3, s32[4,64]{1,0:T(4,128)S(1)} %reshape.162, f32[50,80]{1,0:T(8,128)S(1)} %copy-done.7), kind=kOutput, calls=%fused_computation.12 | convolution fusion | flops 12382720 | bytes 180864 | tf_op jit(solution)/shard_map/tgs,sc->tgc/dot_general | solution.py:89
  (36 shorter events, 0.7 us)
Async XLA Ops:
  0.0 12.2 %copy-start = (bf16[16,16,640]{2,1,0:T(8,128)(2,1)S(1)}, bf16[16,16,640]{2,1,0:T(8,128)(2,1)}, u32[]{:S(2)}) copy-start(bf16[16,16,640]{2,1,0:T(8,128)(2,1)} %param.15) | copy-start | bytes 983044
  0.0 12.0 %copy-start.4 = (bf16[32,640]{1,0:T(8,128)(2,1)S(1)}, bf16[32,640]{1,0:T(8,128)(2,1)}, u32[]{:S(2)}) copy-start(bf16[32,640]{1,0:T(8,128)(2,1)} %param.13) | copy-start | bytes 122884
  0.0 12.1 %copy-start.8 = (s32[2,16]{1,0:T(2,128)S(1)}, s32[2,16]{1,0:T(2,128)}, u32[]{:S(2)}) copy-start(s32[2,16]{1,0:T(2,128)} %param.16) | copy-start | bytes 388
  1.7 43.9 %all-to-all-start = ((bf16[4,640,80]{1,2,0:T(8,128)(2,1)}), bf16[4,640,80]{1,2,0:T(8,128)(2,1)S(1)}, u32[]{:S(2)}, u32[]{:S(2)}) async-start(bf16[4,640,80]{1,2,0:T(8,128)(2,1)} %stack.2), calls=%async_computation | async-start | bytes 819200 | tf_op jit(solution)/shard_map/all_to_all | solution.py:70
  13.6 0.8 %copy-start.5 = (bf16[32,640]{1,0:T(8,128)(2,1)S(1)}, bf16[32,640]{1,0:T(8,128)(2,1)}, u32[]{:S(2)}) copy-start(bf16[32,640]{1,0:T(8,128)(2,1)} %param.12) | copy-start | bytes 122884
  13.6 1.0 %copy-start.2 = (bf16[16,16,640]{2,1,0:T(8,128)(2,1)S(1)}, bf16[16,16,640]{2,1,0:T(8,128)(2,1)}, u32[]{:S(2)}) copy-start(bf16[16,16,640]{2,1,0:T(8,128)(2,1)} %param.14) | copy-start | bytes 983044
  16.0 0.8 %copy-start.6 = (bf16[32,640]{1,0:T(8,128)(2,1)S(1)}, bf16[32,640]{1,0:T(8,128)(2,1)}, u32[]{:S(2)}) copy-start(bf16[32,640]{1,0:T(8,128)(2,1)} %param.11) | copy-start | bytes 122884
  16.0 0.8 %copy-start.9 = (s32[2]{0:T(128)S(1)}, s32[2]{0:T(128)}, u32[]{:S(2)}) copy-start(s32[2]{0:T(128)} %param.17) | copy-start | bytes 28
  46.7 15.8 %copy-start.1 = (s32[128]{0:T(128)S(1)}, s32[128]{0:T(128)}, u32[]{:S(2)}) copy-start(s32[128]{0:T(128)} %param.18) | copy-start | bytes 1540
  47.8 25.7 %all-to-all-start.1 = ((bf16[32,16,4,80]{3,1,2,0:T(8,128)(2,1)}), bf16[32,16,4,80]{3,1,2,0:T(8,128)(2,1)S(1)}, u32[]{:S(2)}, u32[]{:S(2)}) async-start(bf16[32,16,4,80]{3,1,2,0:T(8,128)(2,1)} %bitcast.6), calls=%async_computation.1 | async-start | bytes 1048576 | tf_op jit(solution)/shard_map/all_to_all | solution.py:76
  62.5 11.2 %copy-start.3 = (bf16[4,64,80]{2,1,0:T(8,128)(2,1)S(1)}, bf16[4,64,80]{2,1,0:T(8,128)(2,1)}, u32[]{:S(2)}) copy-start(bf16[4,64,80]{2,1,0:T(8,128)(2,1)} %param.21) | copy-start | bytes 122884
  62.5 11.2 %copy-start.7 = (f32[50,80]{1,0:T(8,128)S(1)}, f32[50,80]{1,0:T(8,128)}, u32[]{:S(2)}) copy-start(f32[50,80]{1,0:T(8,128)} %param.19) | copy-start | bytes 48004
